TPU v7x, 512 devices: a whole 4x4x16 slice. The times are simulated.
512 devices in a mesh: rows: 64 (over y, z), cols: 8 (over x, core).
Axes of the slice: x: 4, y: 4, z: 16, core: 2. Of those that a mesh axis runs over, the one named last changes fastest.
Arguments:
- images: float32 [512, 32, 128], P('rows'), may hold values from -6 to 6
- gauge_pixel: int32 [131072], P('rows'), may hold values from 0 to 32767
- row_mask: int32 [131072], P('rows'), may hold values 0 or 1
- gauge_counts: int32 [64], P('rows'), may hold values from 1 to 2048, as said below
- targets: float32 [131072], P('rows'), may hold values from -10 to 10
- theta: float32 [64, 8], replicated, may hold values from -2.5 to 2.5
- amplitude: float32 [64], replicated, may hold values from 0.5 to 1.5
- damping: float32 [], replicated, may hold values from 0.05 to 0.3
Outputs:
- r_factor: float32 [512, 512], replicated
- new_theta: float32 [64, 8], replicated
- predicted: float32 [131072], P(('rows', 'cols'))
Inputs may be any that keep to these rules, and one draw needn't show every extreme that they name: The slots in use on an index of rows are its first gauge_counts slots; one index of rows uses all 2048.
All inputs are finite; a program needn't handle non-finite values. No bound on the sum of `row_mask` on one device may be relied on, other than what follows from the above.
Results may differ from a plain program's by a relative error of at most 0.0003.
Values sent between devices are 32-bit elements; how exact they have to be, the bound alone decides.
A program may use at most 64 MiB of HBM per device.

v0:
```python
import jax
import jax.numpy as jnp
from jax import lax
from jax.sharding import PartitionSpec as P

BLOCK = 256
y_orders = [0, 1, 0, 2, 1, 0, 0, 0]
x_orders = [0, 0, 1, 0, 1, 2, 0, 2]
sigmas = [1.5, 1.5, 1.5, 1.5, 1.5, 1.5, 3.0, 3.0]


def kernel_values(spacing, deriv_order, width_sigma):
    envelope = jnp.exp(-spacing * spacing / (2.0 * width_sigma * width_sigma))
    if deriv_order == 1:
        return -spacing / width_sigma**2 * envelope
    if deriv_order == 2:
        return (spacing * spacing / width_sigma**4 - 1.0 / width_sigma**2) * envelope
    return envelope


def kernel_table(length, deriv_order, width_sigma):
    places = jnp.arange(length)
    spacing = (places[:, None] - places[None, :]).astype(jnp.float32)
    sample = jnp.arange(-12, 13).astype(jnp.float32)
    scaling = jnp.sqrt(jnp.sum(kernel_values(sample, deriv_order, width_sigma) ** 2))
    return kernel_values(spacing, deriv_order, width_sigma) / scaling


def features(clip_tiles):
    height = clip_tiles.shape[1]
    breadth = clip_tiles.shape[2]
    left_tabs = jnp.stack(
        [kernel_table(height, y_orders[which], sigmas[which]) for which in range(8)]
    )
    right_tabs = jnp.stack(
        [kernel_table(breadth, x_orders[which], sigmas[which]) for which in range(8)]
    )
    partial_conv = jnp.einsum(
        "kij,cjw->kciw", left_tabs, clip_tiles, precision=lax.Precision.HIGHEST
    )
    full_conv = jnp.einsum(
        "kciw,kvw->kciv", partial_conv, right_tabs, precision=lax.Precision.HIGHEST
    )
    return full_conv.reshape(full_conv.shape[0], -1)


def outer_rows(slope, phi):
    return (slope[:, :, None] * phi[:, None, :]).reshape(slope.shape[0], -1)


def solve_step(lower, rhs):
    inner = lax.linalg.triangular_solve(lower, rhs[:, None], left_side=True, lower=True)
    outer = lax.linalg.triangular_solve(lower, inner, left_side=True, lower=True, transpose_a=True)
    return -outer[:, 0]


def on_device(images, gauge_pixel, row_mask, gauge_counts, targets, theta, amplitude, damping):
    ncols = lax.axis_size("cols")
    column = lax.axis_index("cols")
    slots = gauge_pixel.shape[0]
    share = slots // ncols
    channels = theta.shape[0]
    basis_count = theta.shape[1]
    params = channels * basis_count
    local_width = channels // ncols
    own_params = local_width * basis_count
    count = gauge_counts[0]
    live = ((jnp.arange(slots) < count) & (row_mask == 1)).astype(jnp.float32)
    flat_feats = features(images)
    phi = jnp.take(flat_feats, gauge_pixel, axis=1).T
    act = jnp.tanh(jnp.dot(phi, theta.T, precision=lax.Precision.HIGHEST))
    model = jnp.dot(act, amplitude, precision=lax.Precision.HIGHEST)
    resid = live * (model - targets)
    slope = live[:, None] * amplitude[None, :] * (1.0 - act * act)

    def block_rows(values):
        return lax.dynamic_slice_in_dim(values, column * share, share, 0)

    def pick(values):
        return block_rows(values)

    local_slope = lax.dynamic_slice_in_dim(slope, column * local_width, local_width, 1)
    jac_cols = outer_rows(local_slope, phi)
    prefix = jnp.clip(count - column * share, 0, share)
    assigned = lax.all_to_all(jac_cols, "cols", split_axis=0, concat_axis=1, tiled=True)
    assigned_resid = pick(resid)
    trips = (prefix + BLOCK - 1) // BLOCK

    def add_block(which, carry):
        gram = carry[0] + lax.dot_general(
            assigned,
            assigned,
            (((0,), (0,)), ((), ())),
            precision=lax.Precision.HIGHEST,
            preferred_element_type=jnp.float32,
        )
        grad = carry[1] + jnp.dot(assigned_resid, assigned, precision=lax.Precision.HIGHEST)
        return (gram, grad)

    start = (jnp.zeros((params, params), jnp.float32), jnp.zeros((params,), jnp.float32))
    gram_part, grad_part = lax.fori_loop(0, trips, add_block, start)
    live_part = jnp.sum(pick(live))
    gram, grad, total = lax.psum((gram_part, grad_part, live_part), ("rows", "cols"))
    normal = gram / total + damping * jnp.eye(params, dtype=jnp.float32)
    lower = jnp.linalg.cholesky(normal)
    step = solve_step(lower, grad / total)
    local_step = lax.dynamic_slice_in_dim(step, column * own_params, own_params, 0)
    linear_part = lax.psum_scatter(
        jnp.dot(jac_cols, local_step, precision=lax.Precision.HIGHEST),
        "cols",
        scatter_dimension=0,
        tiled=True,
    )
    predicted = block_rows(resid) + linear_part
    return (lower.T, theta + step.reshape(channels, basis_count), predicted)


def solution(mesh):
    return jax.shard_map(
        on_device,
        mesh=mesh,
        in_specs=(P("rows", None, None), P("rows"), P("rows"), P("rows"), P("rows"), P(), P(), P()),
        out_specs=(P(), P(), P(("rows", "cols"))),
        check_vma=False,
    )
```

profile of v0, /device:TPU:8, one launch (start us, length us, event | category | flops | bytes accessed | tf_op | source)
XLA Modules:
  0.0 705.4 jit_solution(6471413244750945603)
XLA Ops:
  18.4 8.6 %copy.61 = f32[8,8,32,128]{0,3,2,1:T(8,128)} copy(f32[8,8,32,128]{3,2,1,0:T(8,128)S(1)} %fusion.15) | data formatting | bytes 2097152 | tf_op jit(solution)/shard_map/reshape | solution.py:44
  27.0 11.2 %gather_fusion = f32[2048,8]{1,0:T(8,128)S(1)} fusion(f32[8,32768]{0,1:T(8,128)} %bitcast.185, s32[2048]{0:T(1024)S(1)} %fusion.50), kind=kCustom, calls=%fused_computation | custom fusion | bytes 139264 | tf_op jit(solution)/shard_map/jit(_take)/gather | solution.py:70
  38.8 1.3 convolution_tanh_fusion
  41.5 4.3 all-to-all-start
  47.1 9.1 %all-to-all-done = f32[8,256,64]{1,2,0:T(8,128)S(1)} async-done(((f32[8,256,64]{1,2,0:T(8,128)}), f32[8,256,64]{1,2,0:T(8,128)S(1)}, u32[]{:S(2)}, u32[]{:S(2)}) %all-to-all-start) | async-done | bytes 524320 | tf_op jit(solution)/shard_map/all_to_all | solution.py:85
  58.2 1.3 copy.45
  62.9 108.7 %all-reduce.2 = (f32[]{:T(128)}, f32[512]{0:T(512)S(1)}) all-reduce(f32[]{:T(128)} %dynamic-slice_reduce_fusion, f32[512]{0:T(512)S(1)} %get-tuple-element.82), channel_id=1, replica_groups=mesh['rows'=64,'cols'=8] {'rows','cols'}, use_global_device_ids=true, to_apply=%region_9.0 | all-reduce | flops 513 | bytes 4104 | tf_op jit(solution)/shard_map/psum | solution.py:103
  172.3 363.3 %all-reduce.5.cloned.1.call-done = f32[512,512]{0,1:T(8,128)} async-done(((f32[512,512]{0,1:T(8,128)}), f32[512,512]{0,1:T(8,128)}) %all-reduce.5.cloned.1.call-update) | async-done | bytes 1048592 | tf_op jit(solution)/shard_map/psum | solution.py:103
  535.6 2.0 select_add_fusion
  537.9 2.1 fusion.12
  540.1 11.7 %cholesky.103 = f32[128,128]{1,0:T(8,128)S(1)} custom-call(f32[128,128]{1,0:T(8,128)S(1)} %cholesky.263), custom_call_target="Cholesky" | custom-call | tf_op jit(solution)/shard_map/jit(cholesky)/cholesky | solution.py:105
  551.8 9.8 %custom-call.32 = f32[1,128,128]{1,2,0:T(8,128)S(1)} custom-call(f32[1,128,128]{2,1,0:T(8,128)S(1)} %get-tuple-element.162), custom_call_target="InvertDiagBlocksLowerTriangular" | custom-call | tf_op jit(solution)/shard_map/jit(cholesky)/cholesky | solution.py:105
  562.3 11.7 %cholesky.215 = f32[128,128]{1,0:T(8,128)S(1)} custom-call(f32[128,128]{1,0:T(8,128)S(1)} %cholesky.267), custom_call_target="Cholesky" | custom-call | tf_op jit(solution)/shard_map/jit(cholesky)/cholesky | solution.py:105
  574.5 9.9 %custom-call.33 = f32[1,128,128]{1,2,0:T(8,128)S(1)} custom-call(f32[1,128,128]{2,1,0:T(8,128)S(1)} %get-tuple-element.160), custom_call_target="InvertDiagBlocksLowerTriangular" | custom-call | tf_op jit(solution)/shard_map/jit(cholesky)/cholesky | solution.py:105
  585.5 11.7 %cholesky.236 = f32[128,128]{1,0:T(8,128)S(1)} custom-call(f32[128,128]{1,0:T(8,128)S(1)} %cholesky.272), custom_call_target="Cholesky" | custom-call | tf_op jit(solution)/shard_map/jit(cholesky)/cholesky | solution.py:105
  597.3 9.8 %custom-call.34 = f32[1,128,128]{1,2,0:T(8,128)S(1)} custom-call(f32[1,128,128]{2,1,0:T(8,128)S(1)} %get-tuple-element.158), custom_call_target="InvertDiagBlocksLowerTriangular" | custom-call | tf_op jit(solution)/shard_map/jit(cholesky)/cholesky | solution.py:105
  607.9 11.9 %cholesky.253 = f32[128,128]{1,0:T(8,128)S(1)} custom-call(f32[128,128]{1,0:T(8,128)S(1)} %convolution_subtract_fusion.2), custom_call_target="Cholesky" | custom-call | tf_op jit(solution)/shard_map/jit(cholesky)/cholesky | solution.py:105
  625.8 11.3 %while.16 = (s32[]{:T(128)}, f32[512,512]{0,1:T(8,128)S(1)}, s32[4,2]{0,1:T(2,128)S(1)}, f32[4,128,128]{2,1,0:T(8,128)}, s32[]{:T(128)}) while((s32[]{:T(128)}, f32[512,512]{0,1:T(8,128)S(1)}, s32[4,2]{0,1:T(2,128)S(1)}, f32[4,128,128]{2,1,0:T(8,128)}, s32[]{:T(128)}) %tuple.61), condition=%wide.while_cond, body=%wide.while_body.sunk | while | flops 2 | bytes 393829 | solution.py:53
  626.4 1.4 dynamic-slice.12
  629.3 1.4 dynamic-slice.12
  632.1 1.4 dynamic-slice.12
  634.9 1.4 dynamic-slice.12
  637.1 40.1 %custom-call.35 = f32[4,128,128]{1,2,0:T(8,128)S(1)} custom-call(f32[4,128,128]{2,1,0:T(8,128)} %get-tuple-element.90), custom_call_target="InvertDiagBlocksLowerTriangular" | custom-call | tf_op jit(solution)/shard_map/triangular_solve | solution.py:53
  681.7 15.2 %all-reduce.1 = f32[2048]{0:T(1024)S(1)} all-reduce(f32[2048]{0:T(1024)S(1)} %bitcast.197), channel_id=2, replica_groups=mesh['rows'=64,'cols'=8] {'cols'}, use_global_device_ids=true, to_apply=%region_19.20.clone | all-reduce | flops 2048 | bytes 16384
  (124 shorter events, 33.4 us)
Async XLA Ops:
  7.2 9.1 %copy-start = (f32[8,32,128]{2,1,0:T(8,128)S(1)}, f32[8,32,128]{2,1,0:T(8,128)}, u32[]{:S(2)}) copy-start(f32[8,32,128]{2,1,0:T(8,128)} %param.10) | copy-start | bytes 393220
  7.2 31.7 %copy-start.1 = (f32[64,8]{0,1:T(8,128)S(1)}, f32[64,8]{0,1:T(8,128)}, u32[]{:S(2)}) copy-start(f32[64,8]{0,1:T(8,128)} %param.15) | copy-start | bytes 6148
  7.2 33.0 %copy-start.3 = (f32[64]{0:T(128)S(1)}, f32[64]{0:T(128)}, u32[]{:S(2)}) copy-start(f32[64]{0:T(128)} %param.16) | copy-start | bytes 772
  7.2 33.1 %copy-start.2 = (s32[2048]{0:T(1024)S(1)}, s32[2048]{0:T(1024)}, u32[]{:S(2)}) copy-start(s32[2048]{0:T(1024)} %param.12) | copy-start | bytes 24580
  41.5 14.6 %all-to-all-start = ((f32[8,256,64]{1,2,0:T(8,128)}), f32[8,256,64]{1,2,0:T(8,128)S(1)}, u32[]{:S(2)}, u32[]{:S(2)}) async-start(f32[8,256,64]{1,2,0:T(8,128)} %copy.43), calls=%async_computation | async-start | bytes 1048576 | tf_op jit(solution)/shard_map/all_to_all | solution.py:85
  45.8 489.8 %all-reduce.5.cloned.1.call-start = ((), (), s32[]{:S(2)}) async-start(), calls=%async_computation.1 | async-start | bytes 2097152 | tf_op jit(solution)/shard_map/psum | solution.py:103
Sparse Core Ops, SparseCore 0:
  59.6 475.9 all-reduce.4
where the time goes:
time: 712 us; the launch traced here: 705 us
  waiting for transfers between devices  372 us (52%)
  other arithmetic  133 us (19%)
  blocking collectives  124 us (17%)
  local copies, waits for them, and re-layouts  37.7 us (5%)
  between operations  22.7 us (3%)
  matrix products  10.9 us (2%)
    psum x1, waiting for transfers between devices, on_device(): lax.psum((gram_part, grad_part, live_part), ('rows', 'cols'))  363 us
    psum x1, blocking collectives, on_device(): lax.psum((gram_part, grad_part, live_part), ('rows', 'cols'))  109 us
    another operation x14, other arithmetic, on_device(): lower = jnp.linalg.cholesky(normal)  78.7 us
    another operation x3, other arithmetic, solve_step(): lax.linalg.triangular_solve(lower, inner, left_side=True, lower=True, tra...  41.4 us
    unnamed x1, blocking collectives  15.2 us
  transfers between devices with their start and end apart: 2, of which 2 were waited for; matrix products, arithmetic and copies ran while one was open for 1% of the time, Pallas kernels for 0%

commit v1 on v0

--- a/solution.py
+++ b/solution.py
@@ -100,7 +100,8 @@
     start = (jnp.zeros((params, params), jnp.float32), jnp.zeros((params,), jnp.float32))
     gram_part, grad_part = lax.fori_loop(0, trips, add_block, start)
     live_part = jnp.sum(pick(live))
-    gram, grad, total = lax.psum((gram_part, grad_part, live_part), ("rows", "cols"))
+    compute_copies_on_mesh = lambda obj: lax.psum(lax.psum(obj, axis_name="rows"), axis_name="cols")
+    gram, grad, total = compute_copies_on_mesh((gram_part, grad_part, live_part))
     normal = gram / total + damping * jnp.eye(params, dtype=jnp.float32)
     lower = jnp.linalg.cholesky(normal)
     step = solve_step(lower, grad / total)

time: 712 us -> 671 us (0.942)
  the two profiles are of different devices: /device:TPU:8 before, /device:TPU:1 now
where the time goes in v1:
time: 671 us; the launch traced here: 664 us
  waiting for transfers between devices  273 us (41%)
  blocking collectives  176 us (26%)
  other arithmetic  133 us (20%)
  local copies, waits for them, and re-layouts  37.7 us (6%)
  between operations  22.7 us (3%)
  matrix products  10.9 us (2%)
  starting transfers between devices  10.3 us (2%)
    psum x1, waiting for transfers between devices, on_device(): lax.psum(obj, axis_name='rows')  264 us
    psum x1, blocking collectives, on_device(): lax.psum(obj, axis_name='rows')  112 us
    another operation x14, other arithmetic, on_device(): lower = jnp.linalg.cholesky(normal)  78.7 us
    psum x1, blocking collectives, on_device(): lax.psum(lax.psum(obj, axis_name='rows'), axis_name='cols')  51.1 us
    another operation x3, other arithmetic, solve_step(): lax.linalg.triangular_solve(lower, inner, left_side=True, lower=True, tra...  41.4 us
  transfers between devices with their start and end apart: 3, of which 2 were waited for; matrix products, arithmetic and copies ran while one was open for 1% of the time, Pallas kernels for 0%

profile of v1, /device:TPU:1, one launch (start us, length us, event | category | flops | bytes accessed | tf_op | source)
XLA Modules:
  0.0 663.9 jit_solution(13950084827675563554)
XLA Ops:
  18.4 8.6 %copy.61 = f32[8,8,32,128]{0,3,2,1:T(8,128)} copy(f32[8,8,32,128]{3,2,1,0:T(8,128)S(1)} %fusion.15) | data formatting | bytes 2097152 | tf_op jit(solution)/shard_map/reshape | solution.py:44
  27.0 11.2 %gather_fusion = f32[2048,8]{1,0:T(8,128)S(1)} fusion(f32[8,32768]{0,1:T(8,128)} %bitcast.185, s32[2048]{0:T(1024)S(1)} %fusion.50), kind=kCustom, calls=%fused_computation | custom fusion | bytes 139264 | tf_op jit(solution)/shard_map/jit(_take)/gather | solution.py:70
  38.8 1.3 convolution_tanh_fusion
  41.5 10.2 %all-to-all-start = ((f32[8,256,64]{1,2,0:T(8,128)}), f32[8,256,64]{1,2,0:T(8,128)S(1)}, u32[]{:S(2)}, u32[]{:S(2)}) async-start(f32[8,256,64]{1,2,0:T(8,128)} %copy.43), calls=%async_computation | async-start | bytes 1048576 | tf_op jit(solution)/shard_map/all_to_all | solution.py:85
  52.9 8.2 %all-to-all-done = f32[8,256,64]{1,2,0:T(8,128)S(1)} async-done(((f32[8,256,64]{1,2,0:T(8,128)}), f32[8,256,64]{1,2,0:T(8,128)S(1)}, u32[]{:S(2)}, u32[]{:S(2)}) %all-to-all-start) | async-done | bytes 524320 | tf_op jit(solution)/shard_map/all_to_all | solution.py:85
  64.6 264.4 %all-reduce.7.cloned.1.call-done = f32[512,512]{0,1:T(8,128)} async-done(((f32[512,512]{0,1:T(8,128)}), f32[512,512]{0,1:T(8,128)}) %all-reduce.7.cloned.1.call-update) | async-done | bytes 1048592 | tf_op jit(solution)/shard_map/psum | solution.py:103
  332.3 112.5 %all-reduce.2 = (f32[]{:T(128)}, f32[512]{0:T(512)S(1)}) all-reduce(f32[]{:T(128)} %dynamic-slice_reduce_fusion, f32[512]{0:T(512)S(1)} %get-tuple-element.82), channel_id=1, replica_groups=mesh['rows'=64,'cols'=8] {'rows'}, use_global_device_ids=true, to_apply=%region_10.0 | all-reduce | flops 513 | bytes 4104 | tf_op jit(solution)/shard_map/psum | solution.py:103
  444.8 51.1 %all-reduce.3 = (f32[]{:T(128)}, f32[512]{0:T(512)S(1)}) all-reduce(f32[]{:T(128)} %get-tuple-element.147, f32[512]{0:T(512)S(1)} %get-tuple-element.148), channel_id=1, replica_groups=mesh['rows'=64,'cols'=8] {'cols'}, use_global_device_ids=true, to_apply=%region_11.0 | all-reduce | flops 513 | bytes 4104 | tf_op jit(solution)/shard_map/psum | solution.py:103
  496.6 2.0 select_add_fusion
  499.0 2.1 fusion.12
  501.1 11.7 %cholesky.103 = f32[128,128]{1,0:T(8,128)S(1)} custom-call(f32[128,128]{1,0:T(8,128)S(1)} %cholesky.263), custom_call_target="Cholesky" | custom-call | tf_op jit(solution)/shard_map/jit(cholesky)/cholesky | solution.py:106
  512.9 9.8 %custom-call.32 = f32[1,128,128]{1,2,0:T(8,128)S(1)} custom-call(f32[1,128,128]{2,1,0:T(8,128)S(1)} %get-tuple-element.164), custom_call_target="InvertDiagBlocksLowerTriangular" | custom-call | tf_op jit(solution)/shard_map/jit(cholesky)/cholesky | solution.py:106
  523.4 11.7 %cholesky.215 = f32[128,128]{1,0:T(8,128)S(1)} custom-call(f32[128,128]{1,0:T(8,128)S(1)} %cholesky.267), custom_call_target="Cholesky" | custom-call | tf_op jit(solution)/shard_map/jit(cholesky)/cholesky | solution.py:106
  535.6 9.9 %custom-call.33 = f32[1,128,128]{1,2,0:T(8,128)S(1)} custom-call(f32[1,128,128]{2,1,0:T(8,128)S(1)} %get-tuple-element.162), custom_call_target="InvertDiagBlocksLowerTriangular" | custom-call | tf_op jit(solution)/shard_map/jit(cholesky)/cholesky | solution.py:106
  546.5 11.7 %cholesky.236 = f32[128,128]{1,0:T(8,128)S(1)} custom-call(f32[128,128]{1,0:T(8,128)S(1)} %cholesky.272), custom_call_target="Cholesky" | custom-call | tf_op jit(solution)/shard_map/jit(cholesky)/cholesky | solution.py:106
  558.4 9.8 %custom-call.34 = f32[1,128,128]{1,2,0:T(8,128)S(1)} custom-call(f32[1,128,128]{2,1,0:T(8,128)S(1)} %get-tuple-element.160), custom_call_target="InvertDiagBlocksLowerTriangular" | custom-call | tf_op jit(solution)/shard_map/jit(cholesky)/cholesky | solution.py:106
  569.0 11.9 %cholesky.253 = f32[128,128]{1,0:T(8,128)S(1)} custom-call(f32[128,128]{1,0:T(8,128)S(1)} %convolution_subtract_fusion.2), custom_call_target="Cholesky" | custom-call | tf_op jit(solution)/shard_map/jit(cholesky)/cholesky | solution.py:106
  586.8 11.3 %while.16 = (s32[]{:T(128)}, f32[512,512]{0,1:T(8,128)S(1)}, s32[4,2]{0,1:T(2,128)S(1)}, f32[4,128,128]{2,1,0:T(8,128)}, s32[]{:T(128)}) while((s32[]{:T(128)}, f32[512,512]{0,1:T(8,128)S(1)}, s32[4,2]{0,1:T(2,128)S(1)}, f32[4,128,128]{2,1,0:T(8,128)}, s32[]{:T(128)}) %tuple.61), condition=%wide.while_cond, body=%wide.while_body.sunk | while | flops 2 | bytes 393829 | solution.py:53
  587.5 1.4 dynamic-slice.12
  590.3 1.4 dynamic-slice.12
  593.1 1.4 dynamic-slice.12
  595.9 1.4 dynamic-slice.12
  598.1 40.1 %custom-call.35 = f32[4,128,128]{1,2,0:T(8,128)S(1)} custom-call(f32[4,128,128]{2,1,0:T(8,128)} %get-tuple-element.90), custom_call_target="InvertDiagBlocksLowerTriangular" | custom-call | tf_op jit(solution)/shard_map/triangular_solve | solution.py:53
  642.8 12.6 %all-reduce.1 = f32[2048]{0:T(1024)S(1)} all-reduce(f32[2048]{0:T(1024)S(1)} %bitcast.197), channel_id=2, replica_groups=mesh['rows'=64,'cols'=8] {'cols'}, use_global_device_ids=true, to_apply=%region_22.23.clone | all-reduce | flops 2048 | bytes 16384
  (128 shorter events, 34.7 us)
Async XLA Ops:
  7.2 9.1 %copy-start = (f32[8,32,128]{2,1,0:T(8,128)S(1)}, f32[8,32,128]{2,1,0:T(8,128)}, u32[]{:S(2)}) copy-start(f32[8,32,128]{2,1,0:T(8,128)} %param.10) | copy-start | bytes 393220
  7.2 31.7 %copy-start.1 = (f32[64,8]{0,1:T(8,128)S(1)}, f32[64,8]{0,1:T(8,128)}, u32[]{:S(2)}) copy-start(f32[64,8]{0,1:T(8,128)} %param.15) | copy-start | bytes 6148
  7.2 33.0 %copy-start.3 = (f32[64]{0:T(128)S(1)}, f32[64]{0:T(128)}, u32[]{:S(2)}) copy-start(f32[64]{0:T(128)} %param.16) | copy-start | bytes 772
  7.2 33.1 %copy-start.2 = (s32[2048]{0:T(1024)S(1)}, s32[2048]{0:T(1024)}, u32[]{:S(2)}) copy-start(s32[2048]{0:T(1024)} %param.12) | copy-start | bytes 24580
  41.5 19.6 %all-to-all-start = ((f32[8,256,64]{1,2,0:T(8,128)}), f32[8,256,64]{1,2,0:T(8,128)S(1)}, u32[]{:S(2)}, u32[]{:S(2)}) async-start(f32[8,256,64]{1,2,0:T(8,128)} %copy.43), calls=%async_computation | async-start | bytes 1048576 | tf_op jit(solution)/shard_map/all_to_all | solution.py:85
  51.8 277.2 %all-reduce.7.cloned.1.call-start = ((), (), s32[]{:S(2)}) async-start(), calls=%async_computation.1 | async-start | bytes 2097152 | tf_op jit(solution)/shard_map/psum | solution.py:103
  64.5 432.1 %all-reduce.9.cloned.1.call-start = ((), (), s32[]{:S(2)}) async-start(), calls=%async_computation.2 | async-start | bytes 2097152 | tf_op jit(solution)/shard_map/psum | solution.py:103
Sparse Core Ops, SparseCore 0:
  64.6 264.2 all-reduce.6
  331.3 81.2 all-reduce.8
